TPU v7x, 32 devices: a whole 2x2x4 slice. The times are simulated.
32 devices in a mesh: mp: 2 (over x), width: 2 (over y), hidden: 8 (over z, core).
Axes of the slice: x: 2, y: 2, z: 4, core: 2. Of those that a mesh axis runs over, the one named last changes fastest.
Arguments:
- residual_in: bfloat16 [2, 512, 3584], P('mp', 'hidden'), may hold values from -6 to 6
- gate_weight: bfloat16 [2, 14336, 3584], P('mp', ('width', 'hidden')), may hold values from -0.09375 to 0.09375
- up_weight: bfloat16 [2, 14336, 3584], P('mp', ('width', 'hidden')), may hold values from -0.09375 to 0.09375
- down_weight: bfloat16 [2, 14336, 3584], P('mp', ('width', 'hidden')), may hold values from -0.046875 to 0.046875
- enc_weight: float32 [7168, 16384], P(('mp', 'width'), 'hidden'), may hold values from -0.0625 to 0.0625
- enc_bias: float32 [16384], P('hidden'), may hold values from -3 to 3
- dec_weight: float32 [16384, 7168], P('hidden', ('mp', 'width')), may hold values from -0.25 to 0.25
- dec_bias: float32 [7168], P(('mp', 'width')), may hold values from -2 to 2
Outputs:
- mlp_acts: bfloat16 [2, 512, 3584], P('mp', 'hidden', 'width')
- latents: float32 [512, 16384], P(None, 'hidden')
- grad_enc: float32 [7168, 16384], P(('mp', 'width'), 'hidden')
- grad_dec: float32 [16384, 7168], P('hidden', ('mp', 'width'))
- grad_enc_bias: float32 [16384], P('hidden')
- grad_dec_bias: float32 [7168], P(('mp', 'width'))
All inputs are finite; a program needn't handle non-finite values.
Results may differ from a plain program's by a relative error of at most 0.0058.
Values may be sent and summed in bfloat16 or wider, within the bound.
A program may use at most 192 MiB of HBM per device.

v0:
```python
import jax
import jax.numpy as jnp
from jax import lax
from jax.sharding import PartitionSpec as P

TOKENS = 512
sharpness = 8.0
sparsity_coef = 0.02
norm_floor = 1e-06
highest = lax.Precision.HIGHEST


def body(
    residual_in, gate_weight, up_weight, down_weight, enc_weight, enc_bias, dec_weight, dec_bias
):
    last_last = (((1,), (1,)), ((), ()))
    first_first = (((0,), (0,)), ((), ()))
    gathered = lax.all_gather(residual_in[0], "hidden", axis=0, tiled=True)
    gate_act = lax.dot_general(
        gathered, gate_weight[0], last_last, preferred_element_type=jnp.float32
    )
    up_act = lax.dot_general(gathered, up_weight[0], last_last, preferred_element_type=jnp.float32)
    hidden_act = (jax.nn.gelu(gate_act, approximate=True) * up_act).astype(jnp.bfloat16)
    down_local = down_weight[0]
    row_sums = lax.psum_scatter(
        jnp.dot(hidden_act, down_local, preferred_element_type=jnp.float32),
        "hidden",
        scatter_dimension=0,
        tiled=True,
    )
    model_sums = lax.psum_scatter(row_sums, "width", scatter_dimension=1, tiled=True)
    mlp_acts = model_sums.astype(jnp.bfloat16)
    coder_in = lax.all_gather(mlp_acts, "hidden", axis=0, tiled=True).astype(jnp.float32)
    enc_partial = jnp.dot(coder_in, enc_weight, precision=highest)
    model_index = lax.axis_index("mp")
    squares = jnp.sum(dec_weight * dec_weight, axis=1)
    square_pair = jnp.where(jnp.arange(2)[:, None] == model_index, squares[None, :], 0.0)
    pre_sum, square_sums = lax.psum((enc_partial, square_pair), ("mp", "width"))
    pre_act = pre_sum + enc_bias
    latents = jax.nn.softplus(sharpness * pre_act) / sharpness
    dec_norms = jnp.sqrt(square_sums + norm_floor)
    recon_part = jnp.dot(latents, dec_weight, precision=highest)
    own_rebuilt = lax.psum_scatter(recon_part, "hidden", scatter_dimension=0, tiled=True) + dec_bias
    own_grad = 2.0 / TOKENS * (own_rebuilt - mlp_acts.astype(jnp.float32))
    err_grad = lax.all_gather(own_grad.astype(jnp.bfloat16), "hidden", axis=0, tiled=True).astype(
        own_grad.dtype
    )
    grad_dec_bias = jnp.sum(err_grad, axis=0)
    back_part = lax.dot_general(
        err_grad, dec_weight, last_last, precision=highest, preferred_element_type=jnp.float32
    )
    lat_grad = lax.psum(back_part.astype(jnp.bfloat16), ("mp", "width")).astype(
        jnp.float32
    ) + sparsity_coef * (dec_norms[0] + dec_norms[1])
    pre_grad = lat_grad * jax.nn.sigmoid(sharpness * pre_act)
    grad_enc_bias = jnp.sum(pre_grad, axis=0)
    grad_enc = lax.dot_general(
        coder_in, pre_grad, first_first, precision=highest, preferred_element_type=jnp.float32
    )
    latent_totals = jnp.sum(latents, axis=0)
    own_norm = jnp.where(model_index == 0, dec_norms[0], dec_norms[1])
    grad_dec = lax.dot_general(
        latents, err_grad, first_first, precision=highest, preferred_element_type=jnp.float32
    )
    grad_dec = grad_dec + sparsity_coef * (latent_totals / own_norm)[:, None] * dec_weight
    return (mlp_acts[None], latents, grad_enc, grad_dec, grad_enc_bias, grad_dec_bias)


def solution(mesh):
    return jax.shard_map(
        body,
        mesh=mesh,
        in_specs=(
            P("mp", "hidden", None),
            P("mp", ("width", "hidden"), None),
            P("mp", ("width", "hidden"), None),
            P("mp", ("width", "hidden"), None),
            P(("mp", "width"), "hidden"),
            P("hidden"),
            P("hidden", ("mp", "width")),
            P(("mp", "width")),
        ),
        out_specs=(
            P("mp", "hidden", "width"),
            P(None, "hidden"),
            P(("mp", "width"), "hidden"),
            P("hidden", ("mp", "width")),
            P("hidden"),
            P(("mp", "width")),
        ),
        check_vma=False,
    )
```

profile of v0, /device:TPU:0, one launch (start us, length us, event | category | flops | bytes accessed | tf_op | source)
XLA Modules:
  0.0 549.1 jit_solution(14673929088239518730)
XLA Ops:
  7.2 0.0 all-gather.9.cloned.1.call-start
  7.2 0.7 all-gather.9.cloned.1.call-update
  7.9 0.0 reduce-scatter.4.cloned.1.call-start
  7.9 47.0 %all-gather.9.cloned.1.call-done = bf16[1,512,3584]{2,1,0:T(8,128)(2,1)} async-done(((bf16[1,64,3584]{2,1,0:T(8,128)(2,1)}), bf16[1,512,3584]{2,1,0:T(8,128)(2,1)}) %all-gather.9.cloned.1.call-update) | async-done | bytes 3670032 | tf_op jit(solution)/shard_map/all_gather | solution.py:18
  54.9 9.6 %fusion.4 = f32[512,896]{1,0:T(8,128)S(1)} fusion(bf16[1,896,3584]{2,1,0:T(8,128)(2,1)} %param.9, bf16[1,512,3584]{2,1,0:T(8,128)(2,1)} %all-gather.9.cloned.1.call-done), kind=kOutput, calls=%fused_computation.7 | convolution fusion | flops 3288334336 | bytes 11927552 | tf_op jit(solution)/shard_map/dot_general | solution.py:19
  64.5 0.0 copy-done.7
  64.6 0.0 slice-start.1
  64.6 7.1 %fusion.17 = bf16[512,896]{1,0:T(8,128)(2,1)S(1)} fusion(f32[512,896]{1,0:T(8,128)S(1)} %fusion.4, bf16[1,896,3584]{2,1,0:T(8,128)(2,1)} %param.10, bf16[1,512,3584]{2,1,0:T(8,128)(2,1)S(1)} %copy-done.7), kind=kOutput, calls=%fused_computation.25 | convolution fusion | flops 3292921856 | bytes 12845056 | tf_op jit(solution)/shard_map/dot_general | solution.py:22
  71.7 0.0 slice-done
  71.7 0.0 slice-done.1
  71.7 6.0 %fusion = f32[512,3584]{1,0:T(8,128)} fusion(bf16[512,896]{1,0:T(8,128)(2,1)S(1)} %fusion.17, bf16[1,896,3584]{2,1,0:T(8,128)(2,1)S(1)} %bitcast.36), kind=kOutput, calls=%fused_computation.3 | convolution fusion | flops 3288334336 | bytes 14680064 | tf_op jit(solution)/shard_map/dot_general | solution.py:26
  77.8 0.0 reduce-scatter.4.cloned.1.call-update
  77.8 0.0 reduce-scatter.6.cloned.1.call-start
  77.9 78.6 %reduce-scatter.4.cloned.1.call-done = f32[64,3584]{1,0:T(8,128)} async-done(((f32[512,3584]{1,0:T(8,128)}), f32[64,3584]{1,0:T(8,128)}) %reduce-scatter.4.cloned.1.call-update) | async-done | bytes 917520 | tf_op jit(solution)/shard_map/reduce_scatter | solution.py:25
  156.4 0.0 reduce-scatter.6.cloned.1.call-update
  156.4 0.0 all-gather.5.cloned.1.call-start
  156.5 19.6 %reduce-scatter.6.cloned.1.call-done = f32[64,1792]{1,0:T(8,128)} async-done(((f32[64,3584]{1,0:T(8,128)}), f32[64,1792]{1,0:T(8,128)}) %reduce-scatter.6.cloned.1.call-update) | async-done | bytes 458768 | tf_op jit(solution)/shard_map/reduce_scatter | solution.py:31
  176.1 1.7 convert_element_type.23
  177.8 0.0 all-gather.5.cloned.1.call-update
  177.9 0.3 all-reduce.3.cloned.1.call-start
  178.2 27.0 %all-gather.5.cloned.1.call-done = bf16[512,1792]{1,0:T(8,128)(2,1)} async-done(((bf16[64,1792]{1,0:T(8,128)(2,1)}), bf16[512,1792]{1,0:T(8,128)(2,1)}) %all-gather.5.cloned.1.call-update) | async-done | bytes 1835024 | tf_op jit(solution)/shard_map/all_gather | solution.py:33
  205.2 16.9 %fusion.26 = f32[512,2048]{1,0:T(8,128)} fusion(bf16[512,1792]{1,0:T(8,128)(2,1)} %all-gather.5.cloned.1.call-done, f32[1792,2048]{1,0:T(8,128)} %param.12), kind=kOutput, calls=%fused_computation.36 | convolution fusion | flops 22548578304 | bytes 20709376 | tf_op jit(solution)/shard_map/dot_general | solution.py:34
  222.1 0.0 all-reduce.3.cloned.1.call-update
  222.1 0.4 reduce-scatter.8.cloned.1.call-start
  222.5 102.8 %all-reduce.3.cloned.1.call-done = f32[512,2048]{1,0:T(8,128)} async-done(((f32[512,2048]{1,0:T(8,128)}), f32[512,2048]{1,0:T(8,128)}) %all-reduce.3.cloned.1.call-update) | async-done | bytes 4194320 | tf_op jit(solution)/shard_map/psum | solution.py:38
  325.3 4.9 fusion.24
  330.2 0.0 copy-start
  330.2 2.0 copy-done
  332.2 26.6 %fusion.27 = f32[512,1792]{1,0:T(8,128)} fusion(f32[512,2048]{1,0:T(8,128)S(1)} %get-tuple-element.7, f32[2048,1792]{1,0:T(8,128)} %param.14), kind=kOutput, calls=%fused_computation.37 | convolution fusion | flops 22548578304 | bytes 22544384 | tf_op jit(solution)/shard_map/dot_general | solution.py:42
  358.9 0.0 reduce-scatter.8.cloned.1.call-update
  358.9 0.0 all-gather.7.cloned.1.call-start
  359.0 45.1 %reduce-scatter.8.cloned.1.call-done = f32[64,1792]{1,0:T(8,128)} async-done(((f32[512,1792]{1,0:T(8,128)}), f32[64,1792]{1,0:T(8,128)}) %reduce-scatter.8.cloned.1.call-update) | async-done | bytes 458768 | tf_op jit(solution)/shard_map/reduce_scatter | solution.py:43
  404.0 0.0 copy-done.6
  404.1 1.8 multiply_convert_fusion
  405.8 0.0 all-gather.7.cloned.1.call-update
  405.8 0.0 all-reduce.5.cloned.1.call-start
  405.9 6.2 %multiply_reduce_fusion = f32[2048]{0:T(1024)S(1)} fusion(f32[2048,1792]{1,0:T(8,128)} %param.14), kind=kLoop, calls=%fused_computation.1 | loop fusion | flops 7337984 | bytes 14688256 | tf_op jit(solution)/shard_map/reduce_sum | solution.py:36
  412.1 0.1 broadcast_select_fusion
  412.2 16.5 %psum.23 = f32[2,2048]{1,0:T(2,128)S(1)} all-reduce(f32[2,2048]{1,0:T(2,128)S(1)} %broadcast_select_fusion), channel_id=1, replica_groups=mesh['mp'=2,'width'=2,'hidden'=8] {'mp','width'}, use_global_device_ids=true, to_apply=%region_6.7 | all-reduce | flops 4096 | bytes 32768 | tf_op jit(solution)/shard_map/psum | solution.py:38
  428.8 2.9 all-gather.7.cloned.1.call-done
  431.7 18.4 %convolution_convert_fusion = bf16[512,2048]{1,0:T(8,128)(2,1)} fusion(bf16[512,1792]{1,0:T(8,128)(2,1)} %all-gather.7.cloned.1.call-done, f32[2048,1792]{1,0:T(8,128)} %param.14), kind=kOutput, calls=%fused_computation.15 | convolution fusion | flops 22549626880 | bytes 18612224 | tf_op jit(solution)/shard_map/dot_general | solution.py:49
  450.1 0.0 all-reduce.5.cloned.1.call-update
  450.1 0.7 convert_bitcast_fusion
  450.8 0.9 convert_reduce_fusion
  451.7 19.6 %multiply_add_fusion = f32[2048,1792]{1,0:T(8,128)} fusion(f32[2048,1792]{1,0:T(8,128)} %param.14, f32[512,2048]{1,0:T(8,128)} %copy-done, bf16[512,1792]{1,0:T(8,128)(2,1)S(1)} %copy-done.2, f32[2048]{0:T(1024)S(1)} %divide_multiply_fusion.1), kind=kOutput, calls=%fused_computation | convolution fusion | flops 22555918336 | bytes 35397632 | tf_op jit(solution)/shard_map/dot_general | solution.py:62
  471.3 47.8 %all-reduce.5.cloned.1.call-done = bf16[512,2048]{1,0:T(8,128)(2,1)} async-done(((bf16[512,2048]{1,0:T(8,128)(2,1)}), bf16[512,2048]{1,0:T(8,128)(2,1)}) %all-reduce.5.cloned.1.call-update) | async-done | bytes 2097168 | tf_op jit(solution)/shard_map/psum | solution.py:52
  519.2 5.0 fusion.22
  524.1 17.9 %fusion.23 = f32[1792,2048]{1,0:T(8,128)} fusion(bf16[512,1792]{1,0:T(8,128)(2,1)} %all-gather.5.cloned.1.call-done, bf16[512,2048]{1,0:T(8,128)(2,1)S(1)} %copy-done.4, f32[512,2048]{1,0:T(8,128)S(1)} %copy-done.1, f32[2048]{0:T(1024)S(1)} %bitcast.33, f32[2048]{0:T(1024)S(1)} %copy-done.5), kind=kOutput, calls=%fused_computation.34 | convolution fusion | flops 22556966912 | bytes 22822912 | tf_op jit(solution)/shard_map/dot_general | solution.py:57
  (18 shorter events, 0.1 us)
Async XLA Ops:
  7.2 47.7 %all-gather.9.cloned.1.call-start = ((), (), s32[]{:S(2)}) async-start(), calls=%async_computation.10 | async-start | bytes 4128768 | tf_op jit(solution)/shard_map/all_gather | solution.py:18
  7.9 148.5 %reduce-scatter.4.cloned.1.call-start = ((), (), s32[]{:S(2)}) async-start(), calls=%async_computation.3 | async-start | bytes 8257536 | tf_op jit(solution)/shard_map/reduce_scatter | solution.py:25
  54.9 9.6 %copy-start.7 = (bf16[1,512,3584]{2,1,0:T(8,128)(2,1)S(1)}, bf16[1,512,3584]{2,1,0:T(8,128)(2,1)}, u32[]{:S(2)}) copy-start(bf16[1,512,3584]{2,1,0:T(8,128)(2,1)} %all-gather.9.cloned.1.call-done) | copy-start | bytes 11010052
  54.9 16.8 %slice-start = ((s8[6422528]{0:T(1024)(128)(4,1)}), s8[4194304]{0:T(1024)(128)(4,1)S(1)}, s32[]{:S(2)}) async-start(s8[6422528]{0:T(1024)(128)(4,1)} %bitcast.35), calls=%async_computation.11 | async-start | bytes 8388608
  64.6 7.2 %slice-start.1 = ((s8[6422528]{0:T(1024)(128)(4,1)}), s8[2228224]{0:T(1024)(128)(4,1)S(1)}, s32[]{:S(2)}) async-start(s8[6422528]{0:T(1024)(128)(4,1)} %bitcast.35), calls=%async_computation.12 | async-start | bytes 4456448
  77.8 98.3 %reduce-scatter.6.cloned.1.call-start = ((), (), s32[]{:S(2)}) async-start(), calls=%async_computation.4 | async-start | bytes 1376256 | tf_op jit(solution)/shard_map/reduce_scatter | solution.py:31
  156.4 48.8 %all-gather.5.cloned.1.call-start = ((), (), s32[]{:S(2)}) async-start(), calls=%async_computation.5 | async-start | bytes 2064384 | tf_op jit(solution)/shard_map/all_gather | solution.py:33
  177.9 147.4 %all-reduce.3.cloned.1.call-start = ((), (), s32[]{:S(2)}) async-start(), calls=%async_computation.6 | async-start | bytes 8388608 | tf_op jit(solution)/shard_map/psum | solution.py:38
  222.1 103.2 %copy-start.5 = (f32[2048]{0:T(1024)S(1)}, f32[2048]{0:T(1024)}, u32[]{:S(2)}) copy-start(f32[2048]{0:T(1024)} %param.13) | copy-start | bytes 24580
  222.1 181.9 %reduce-scatter.8.cloned.1.call-start = ((), (), s32[]{:S(2)}) async-start(), calls=%async_computation.7 | async-start | bytes 4128768 | tf_op jit(solution)/shard_map/reduce_scatter | solution.py:43
  330.2 2.0 copy-start
  332.2 71.8 %copy-start.3 = (f32[64,1792]{1,0:T(8,128)S(1)}, f32[64,1792]{1,0:T(8,128)}, u32[]{:S(2)}) copy-start(f32[64,1792]{1,0:T(8,128)} %reduce-scatter.6.cloned.1.call-done) | copy-start | bytes 1376260
  332.2 71.8 %copy-start.6 = (f32[1792]{0:T(1024)S(1)}, f32[1792]{0:T(1024)}, u32[]{:S(2)}) copy-start(f32[1792]{0:T(1024)} %param.15) | copy-start | bytes 21508
  358.9 72.7 %all-gather.7.cloned.1.call-start = ((), (), s32[]{:S(2)}) async-start(), calls=%async_computation.8 | async-start | bytes 2064384 | tf_op jit(solution)/shard_map/all_gather | solution.py:45
  405.8 113.3 %all-reduce.5.cloned.1.call-start = ((), (), s32[]{:S(2)}) async-start(), calls=%async_computation.9 | async-start | bytes 4194304 | tf_op jit(solution)/shard_map/psum | solution.py:52
  431.7 19.2 %copy-start.2 = (bf16[512,1792]{1,0:T(8,128)(2,1)S(1)}, bf16[512,1792]{1,0:T(8,128)(2,1)}, u32[]{:S(2)}) copy-start(bf16[512,1792]{1,0:T(8,128)(2,1)} %all-gather.7.cloned.1.call-done) | copy-start | bytes 5505028
  519.1 5.0 copy-start.1
  519.1 5.0 copy-start.4
Sparse Core Ops, SparseCore 0:
  9.6 45.2 all-gather.8
  77.9 78.4 reduce-scatter.3
  158.7 17.3 reduce-scatter.5
  178.2 26.9 all-gather.4
  222.2 103.0 all-reduce.2
  359.0 44.9 reduce-scatter.7
  406.3 25.3 all-gather.6
  450.2 68.8 all-reduce.4
where the time goes:
time: 555 us; the launch traced here: 549 us
  waiting for transfers between devices  372 us (67%)
  matrix products  122 us (22%)
  other arithmetic  21.3 us (4%)
  blocking collectives  16.5 us (3%)
  between operations  14.5 us (3%)
    psum x1, waiting for transfers between devices, body(): pre_sum, square_sums = lax.psum((enc_partial, square_pair), ('mp', 'width'))  103 us
    reduce_scatter x1, waiting for transfers between devices, body(): lax.psum_scatter(jnp.dot(hidden_act, down_local, preferred_element_type=j...  78.6 us
    psum x1, waiting for transfers between devices, body(): lax.psum(back_part.astype(jnp.bfloat16), ('mp', 'width'))  47.8 us
    all_gather x1, waiting for transfers between devices, body(): gathered = lax.all_gather(residual_in[0], 'hidden', axis=0, tiled=True)  47 us
    reduce_scatter x1, waiting for transfers between devices, body(): lax.psum_scatter(recon_part, 'hidden', scatter_dimension=0, tiled=True)  45.1 us
    all_gather x1, waiting for transfers between devices, body(): lax.all_gather(mlp_acts, 'hidden', axis=0, tiled=True).astype(jnp.float32)  27 us
    dot_general x1, matrix products, body(): recon_part = jnp.dot(latents, dec_weight, precision=highest)  26.6 us
    reduce_scatter x1, waiting for transfers between devices, body(): lax.psum_scatter(row_sums, 'width', scatter_dimension=1, tiled=True)  19.6 us
  transfers between devices with their start and end apart: 8, of which 8 were waited for; matrix products, arithmetic and copies ran while one was open for 5% of the time, Pallas kernels for 0%

commit v1 on v0

--- a/solution.py
+++ b/solution.py
@@ -49,9 +49,9 @@
     back_part = lax.dot_general(
         err_grad, dec_weight, last_last, precision=highest, preferred_element_type=jnp.float32
     )
-    lat_grad = lax.psum(back_part.astype(jnp.bfloat16), ("mp", "width")).astype(
-        jnp.float32
-    ) + sparsity_coef * (dec_norms[0] + dec_norms[1])
+    lat_grad = jnp.sum(
+        lax.all_gather(back_part.astype(jnp.bfloat16), ("mp", "width")), axis=0
+    ).astype(jnp.float32) + sparsity_coef * (dec_norms[0] + dec_norms[1])
     pre_grad = lat_grad * jax.nn.sigmoid(sharpness * pre_act)
     grad_enc_bias = jnp.sum(pre_grad, axis=0)
     grad_enc = lax.dot_general(

time: 555 us -> 574 us (1.034)
  waiting for transfers between devices: 372 us -> 390 us
    psum x1 -> x0, waiting for transfers between devices: 47.8 us -> none  [body(): lax.psum(back_part.astype(jnp.bfloat16), ('mp', 'width'))]
    all_gather x0 -> x1, waiting for transfers between devices: none -> 43.3 us  [body(): lax.all_gather(back_part.astype(jnp.bfloat16), ('mp', 'width'))]
    all_gather x1, waiting for transfers between devices: 2.86 us -> 25.6 us  [body(): lax.all_gather(own_grad.astype(jnp.bfloat16), 'hidden', axis=0, tiled=True)]
where the time goes in v1:
time: 574 us; the launch traced here: 569 us
  waiting for transfers between devices  390 us (68%)
  matrix products  117 us (20%)
  other arithmetic  26.5 us (5%)
  blocking collectives  17.1 us (3%)
  between operations  14.8 us (3%)
    psum x1, waiting for transfers between devices, body(): pre_sum, square_sums = lax.psum((enc_partial, square_pair), ('mp', 'width'))  103 us
    reduce_scatter x1, waiting for transfers between devices, body(): lax.psum_scatter(jnp.dot(hidden_act, down_local, preferred_element_type=j...  78.6 us
    all_gather x1, waiting for transfers between devices, body(): gathered = lax.all_gather(residual_in[0], 'hidden', axis=0, tiled=True)  47 us
    reduce_scatter x1, waiting for transfers between devices, body(): lax.psum_scatter(recon_part, 'hidden', scatter_dimension=0, tiled=True)  45.1 us
    all_gather x1, waiting for transfers between devices, body(): lax.all_gather(back_part.astype(jnp.bfloat16), ('mp', 'width'))  43.3 us
    all_gather x1, waiting for transfers between devices, body(): lax.all_gather(mlp_acts, 'hidden', axis=0, tiled=True).astype(jnp.float32)  26.8 us
    dot_general x1, matrix products, body(): recon_part = jnp.dot(latents, dec_weight, precision=highest)  26.6 us
    all_gather x1, waiting for transfers between devices, body(): lax.all_gather(own_grad.astype(jnp.bfloat16), 'hidden', axis=0, tiled=True)  25.6 us
  transfers between devices with their start and end apart: 8, of which 8 were waited for; matrix products, arithmetic and copies ran while one was open for 5% of the time, Pallas kernels for 0%

profile of v1, /device:TPU:0, one launch (start us, length us, event | category | flops | bytes accessed | tf_op | source)
XLA Modules:
  0.0 568.7 jit_solution(1703292987378138539)
XLA Ops:
  7.2 0.0 all-gather.11.cloned.1.call-start
  7.2 0.7 all-gather.11.cloned.1.call-update
  7.9 0.0 reduce-scatter.4.cloned.1.call-start
  7.9 47.0 %all-gather.11.cloned.1.call-done = bf16[1,512,3584]{2,1,0:T(8,128)(2,1)} async-done(((bf16[1,64,3584]{2,1,0:T(8,128)(2,1)}), bf16[1,512,3584]{2,1,0:T(8,128)(2,1)}) %all-gather.11.cloned.1.call-update) | async-done | bytes 3670032 | tf_op jit(solution)/shard_map/all_gather | solution.py:18
  54.9 9.6 %fusion.4 = f32[512,896]{1,0:T(8,128)S(1)} fusion(bf16[1,896,3584]{2,1,0:T(8,128)(2,1)} %param.9, bf16[1,512,3584]{2,1,0:T(8,128)(2,1)} %all-gather.11.cloned.1.call-done), kind=kOutput, calls=%fused_computation.7 | convolution fusion | flops 3288334336 | bytes 11927552 | tf_op jit(solution)/shard_map/dot_general | solution.py:19
  64.6 0.0 slice-start.1
  64.6 7.1 %fusion.17 = bf16[512,896]{1,0:T(8,128)(2,1)S(1)} fusion(f32[512,896]{1,0:T(8,128)S(1)} %fusion.4, bf16[1,896,3584]{2,1,0:T(8,128)(2,1)} %param.10, bf16[1,512,3584]{2,1,0:T(8,128)(2,1)S(1)} %copy-done.6), kind=kOutput, calls=%fused_computation.25 | convolution fusion | flops 3292921856 | bytes 12845056 | tf_op jit(solution)/shard_map/dot_general | solution.py:22
  71.7 0.0 slice-done
  71.7 0.0 slice-done.1
  71.7 6.0 %fusion = f32[512,3584]{1,0:T(8,128)} fusion(bf16[512,896]{1,0:T(8,128)(2,1)S(1)} %fusion.17, bf16[1,896,3584]{2,1,0:T(8,128)(2,1)S(1)} %bitcast.38), kind=kOutput, calls=%fused_computation.3 | convolution fusion | flops 3288334336 | bytes 14680064 | tf_op jit(solution)/shard_map/dot_general | solution.py:26
  77.8 0.0 reduce-scatter.4.cloned.1.call-update
  77.8 0.0 reduce-scatter.6.cloned.1.call-start
  77.9 78.6 %reduce-scatter.4.cloned.1.call-done = f32[64,3584]{1,0:T(8,128)} async-done(((f32[512,3584]{1,0:T(8,128)}), f32[64,3584]{1,0:T(8,128)}) %reduce-scatter.4.cloned.1.call-update) | async-done | bytes 917520 | tf_op jit(solution)/shard_map/reduce_scatter | solution.py:25
  156.4 0.0 reduce-scatter.6.cloned.1.call-update
  156.4 0.0 all-gather.7.cloned.1.call-start
  156.5 19.6 %reduce-scatter.6.cloned.1.call-done = f32[64,1792]{1,0:T(8,128)} async-done(((f32[64,3584]{1,0:T(8,128)}), f32[64,1792]{1,0:T(8,128)}) %reduce-scatter.6.cloned.1.call-update) | async-done | bytes 458768 | tf_op jit(solution)/shard_map/reduce_scatter | solution.py:31
  176.1 1.7 convert_element_type.25
  177.8 0.0 all-gather.7.cloned.1.call-update
  177.9 0.6 all-reduce.2.cloned.1.call-start
  178.4 26.8 %all-gather.7.cloned.1.call-done = bf16[512,1792]{1,0:T(8,128)(2,1)} async-done(((bf16[64,1792]{1,0:T(8,128)(2,1)}), bf16[512,1792]{1,0:T(8,128)(2,1)}) %all-gather.7.cloned.1.call-update) | async-done | bytes 1835024 | tf_op jit(solution)/shard_map/all_gather | solution.py:33
  205.2 16.9 %fusion.26 = f32[512,2048]{1,0:T(8,128)} fusion(bf16[512,1792]{1,0:T(8,128)(2,1)} %all-gather.7.cloned.1.call-done, f32[1792,2048]{1,0:T(8,128)} %param.12), kind=kOutput, calls=%fused_computation.36 | convolution fusion | flops 22548578304 | bytes 20709376 | tf_op jit(solution)/shard_map/dot_general | solution.py:34
  222.1 0.0 all-reduce.2.cloned.1.call-update
  222.1 0.2 reduce-scatter.8.cloned.1.call-start
  222.3 103.0 %all-reduce.2.cloned.1.call-done = f32[512,2048]{1,0:T(8,128)} async-done(((f32[512,2048]{1,0:T(8,128)}), f32[512,2048]{1,0:T(8,128)}) %all-reduce.2.cloned.1.call-update) | async-done | bytes 4194320 | tf_op jit(solution)/shard_map/psum | solution.py:38
  325.3 0.0 copy-done.4
  325.3 4.9 fusion.24
  330.2 0.0 copy-start
  330.2 2.0 copy-done
  332.2 26.6 %fusion.27 = f32[512,1792]{1,0:T(8,128)} fusion(f32[512,2048]{1,0:T(8,128)S(1)} %get-tuple-element.7, f32[2048,1792]{1,0:T(8,128)} %param.14), kind=kOutput, calls=%fused_computation.37 | convolution fusion | flops 22548578304 | bytes 22544384 | tf_op jit(solution)/shard_map/dot_general | solution.py:42
  358.9 0.0 reduce-scatter.8.cloned.1.call-update
  358.9 0.0 all-gather.9.cloned.1.call-start
  359.0 45.1 %reduce-scatter.8.cloned.1.call-done = f32[64,1792]{1,0:T(8,128)} async-done(((f32[512,1792]{1,0:T(8,128)}), f32[64,1792]{1,0:T(8,128)}) %reduce-scatter.8.cloned.1.call-update) | async-done | bytes 458768 | tf_op jit(solution)/shard_map/reduce_scatter | solution.py:43
  404.0 1.8 multiply_convert_fusion
  405.8 0.0 all-gather.9.cloned.1.call-update
  405.8 0.3 all-gather.13.cloned.1.call-start
  406.1 25.6 %all-gather.9.cloned.1.call-done = bf16[512,1792]{1,0:T(8,128)(2,1)} async-done(((bf16[64,1792]{1,0:T(8,128)(2,1)}), bf16[512,1792]{1,0:T(8,128)(2,1)}) %all-gather.9.cloned.1.call-update) | async-done | bytes 1835024 | tf_op jit(solution)/shard_map/all_gather | solution.py:45
  431.7 16.5 %convolution_convert_fusion = bf16[512,2048]{1,0:T(8,128)(2,1)} fusion(bf16[512,1792]{1,0:T(8,128)(2,1)} %all-gather.9.cloned.1.call-done, f32[2048,1792]{1,0:T(8,128)} %param.14), kind=kOutput, calls=%fused_computation.15 | convolution fusion | flops 22549626880 | bytes 18612224 | tf_op jit(solution)/shard_map/dot_general | solution.py:49
  448.2 0.0 all-gather.13.cloned.1.call-update
  448.3 6.3 %multiply_reduce_fusion = f32[2048]{0:T(1024)S(1)} fusion(f32[2048,1792]{1,0:T(8,128)} %param.14), kind=kLoop, calls=%fused_computation.1 | loop fusion | flops 7337984 | bytes 14688256 | tf_op jit(solution)/shard_map/reduce_sum | solution.py:36
  454.6 0.1 broadcast_select_fusion
  454.7 17.1 %psum.15 = f32[2,2048]{1,0:T(2,128)S(1)} all-reduce(f32[2,2048]{1,0:T(2,128)S(1)} %broadcast_select_fusion), channel_id=1, replica_groups=mesh['mp'=2,'width'=2,'hidden'=8] {'mp','width'}, use_global_device_ids=true, to_apply=%region_6.7 | all-reduce | flops 4096 | bytes 32768 | tf_op jit(solution)/shard_map/psum | solution.py:38
  471.9 0.7 convert_bitcast_fusion
  472.6 0.9 convert_reduce_fusion
  473.5 18.9 %multiply_add_fusion = f32[2048,1792]{1,0:T(8,128)} fusion(f32[2048,1792]{1,0:T(8,128)} %param.14, f32[512,2048]{1,0:T(8,128)} %copy-done, bf16[512,1792]{1,0:T(8,128)(2,1)S(1)} %copy-done.2, f32[2048]{0:T(1024)S(1)} %divide_multiply_fusion.1), kind=kOutput, calls=%fused_computation | convolution fusion | flops 22555918336 | bytes 35397632 | tf_op jit(solution)/shard_map/dot_general | solution.py:62
  492.4 43.3 %all-gather.13.cloned.1.call-done = bf16[2048,2048]{1,0:T(8,128)(2,1)} async-done(((bf16[512,2048]{1,0:T(8,128)(2,1)}), bf16[2048,2048]{1,0:T(8,128)(2,1)}) %all-gather.13.cloned.1.call-update) | async-done | bytes 8388624 | tf_op jit(solution)/shard_map/all_gather | solution.py:53
  535.7 5.7 reduce_sum.48
  541.4 4.3 fusion.22
  545.7 15.6 %fusion.23 = f32[1792,2048]{1,0:T(8,128)} fusion(bf16[512,1792]{1,0:T(8,128)(2,1)S(1)} %copy-done.7, bf16[512,2048]{1,0:T(8,128)(2,1)S(1)} %reduce_sum.48, f32[512,2048]{1,0:T(8,128)S(1)} %copy-done.1, f32[2048]{0:T(1024)S(1)} %bitcast.35, f32[2048]{0:T(1024)S(1)} %copy-done.4), kind=kOutput, calls=%fused_computation.34 | convolution fusion | flops 22556966912 | bytes 22822912 | tf_op jit(solution)/shard_map/dot_general | solution.py:57
  (19 shorter events, 0.1 us)
Async XLA Ops:
  7.2 47.7 %all-gather.11.cloned.1.call-start = ((), (), s32[]{:S(2)}) async-start(), calls=%async_computation.9 | async-start | bytes 4128768 | tf_op jit(solution)/shard_map/all_gather | solution.py:18
  7.9 148.5 %reduce-scatter.4.cloned.1.call-start = ((), (), s32[]{:S(2)}) async-start(), calls=%async_computation.3 | async-start | bytes 8257536 | tf_op jit(solution)/shard_map/reduce_scatter | solution.py:25
  54.9 9.6 %copy-start.6 = (bf16[1,512,3584]{2,1,0:T(8,128)(2,1)S(1)}, bf16[1,512,3584]{2,1,0:T(8,128)(2,1)}, u32[]{:S(2)}) copy-start(bf16[1,512,3584]{2,1,0:T(8,128)(2,1)} %all-gather.11.cloned.1.call-done) | copy-start | bytes 11010052
  54.9 16.8 %slice-start = ((s8[6422528]{0:T(1024)(128)(4,1)}), s8[4194304]{0:T(1024)(128)(4,1)S(1)}, s32[]{:S(2)}) async-start(s8[6422528]{0:T(1024)(128)(4,1)} %bitcast.37), calls=%async_computation.11 | async-start | bytes 8388608
  64.6 7.2 %slice-start.1 = ((s8[6422528]{0:T(1024)(128)(4,1)}), s8[2228224]{0:T(1024)(128)(4,1)S(1)}, s32[]{:S(2)}) async-start(s8[6422528]{0:T(1024)(128)(4,1)} %bitcast.37), calls=%async_computation.12 | async-start | bytes 4456448
  77.8 98.3 %reduce-scatter.6.cloned.1.call-start = ((), (), s32[]{:S(2)}) async-start(), calls=%async_computation.4 | async-start | bytes 1376256 | tf_op jit(solution)/shard_map/reduce_scatter | solution.py:31
  156.4 48.8 %all-gather.7.cloned.1.call-start = ((), (), s32[]{:S(2)}) async-start(), calls=%async_computation.5 | async-start | bytes 2064384 | tf_op jit(solution)/shard_map/all_gather | solution.py:33
  177.9 147.5 %all-reduce.2.cloned.1.call-start = ((), (), s32[]{:S(2)}) async-start(), calls=%async_computation.6 | async-start | bytes 8388608 | tf_op jit(solution)/shard_map/psum | solution.py:38
  222.1 103.2 %copy-start.4 = (f32[2048]{0:T(1024)S(1)}, f32[2048]{0:T(1024)}, u32[]{:S(2)}) copy-start(f32[2048]{0:T(1024)} %param.13) | copy-start | bytes 24580
  222.1 181.9 %reduce-scatter.8.cloned.1.call-start = ((), (), s32[]{:S(2)}) async-start(), calls=%async_computation.7 | async-start | bytes 4128768 | tf_op jit(solution)/shard_map/reduce_scatter | solution.py:43
  330.2 2.0 copy-start
  332.2 71.8 %copy-start.3 = (f32[64,1792]{1,0:T(8,128)S(1)}, f32[64,1792]{1,0:T(8,128)}, u32[]{:S(2)}) copy-start(f32[64,1792]{1,0:T(8,128)} %reduce-scatter.6.cloned.1.call-done) | copy-start | bytes 1376260
  332.2 71.8 %copy-start.5 = (f32[1792]{0:T(1024)S(1)}, f32[1792]{0:T(1024)}, u32[]{:S(2)}) copy-start(f32[1792]{0:T(1024)} %param.15) | copy-start | bytes 21508
  358.9 72.7 %all-gather.9.cloned.1.call-start = ((), (), s32[]{:S(2)}) async-start(), calls=%async_computation.8 | async-start | bytes 2064384 | tf_op jit(solution)/shard_map/all_gather | solution.py:45
  405.8 129.8 %all-gather.13.cloned.1.call-start = ((), (), s32[]{:S(2)}) async-start(), calls=%async_computation.10 | async-start | bytes 10485760 | tf_op jit(solution)/shard_map/all_gather | solution.py:53
  448.2 24.3 %copy-start.2 = (bf16[512,1792]{1,0:T(8,128)(2,1)S(1)}, bf16[512,1792]{1,0:T(8,128)(2,1)}, u32[]{:S(2)}) copy-start(bf16[512,1792]{1,0:T(8,128)(2,1)} %all-gather.9.cloned.1.call-done) | copy-start | bytes 5505028
  541.4 4.3 copy-start.1
  541.4 4.3 copy-start.7
Sparse Core Ops, SparseCore 0:
  9.6 45.2 all-gather.10
  77.9 78.4 reduce-scatter.3
  158.7 17.3 reduce-scatter.5
  178.2 26.9 all-gather.6
  222.2 103.0 all-reduce.1
  359.0 44.9 reduce-scatter.7
  406.2 25.3 all-gather.8
  448.3 87.2 all-gather.12
